TPU v7x, 32 devices: a whole 2x2x4 slice. The times are simulated.
32 devices in a mesh: grp: 2 (over x), ctx: 16 (over z, y, core).
Axes of the slice: x: 2, y: 2, z: 4, core: 2. Of those that a mesh axis runs over, the one named last changes fastest.
Arguments:
- queries: bfloat16 [8192, 8192], P(('grp', 'ctx')), parts along dimension 0, may hold values from -14 to 14
- keys: bfloat16 [8192, 1024], P(('grp', 'ctx')), parts along dimension 0, may hold values from -14 to 14
- values: bfloat16 [8192, 1024], P(('grp', 'ctx')), parts along dimension 0, may hold values from -6 to 6
- lengths: int32 [32], P(('grp', 'ctx')), parts along dimension 0, may hold values from 64 to 256, as said below
Outputs:
- attended: bfloat16 [8192, 8192], P(('grp', 'ctx')), parts along dimension 0
There are 2 independent parts, one for each index of `grp`. A program takes and returns all parts, laid end to end along the dimension named above; each array names one. Nothing has to cross between parts.
Inputs may be any that keep to these rules, and one draw needn't show every extreme that they name: `lengths`: block 0 is always full (256 valid tokens).
All inputs are finite; a program needn't handle non-finite values.
Results may differ from a plain program's by a relative error of at most 0.006.
Values may be sent and summed in bfloat16 or wider, within the bound.
No kernel may reach another device: no remote copies, remote signals or barrier semaphores. Data moves between devices by JAX's collectives and lax.ppermute only.
A program may use at most 128 MiB of HBM per device.

v0:
```python
import math

import jax
import jax.numpy as jnp
from jax import lax
from jax.sharding import PartitionSpec as P

HD = 128
ANCHOR = 256


rope_base = 500000.0
old_context = 8192.0
scale_factor = 8.0
low_factor = 1.0
high_factor = 4.0
masked_score = -1e30


def spread(block, axis, source):
    block = jnp.where(lax.axis_index(axis) == source, block, jnp.zeros_like(block))
    return lax.psum(block, axis)


def frequencies(head_dim):
    half_size = head_dim // 2
    inverse = rope_base ** (-2.0 * jnp.arange(half_size, dtype=jnp.float32) / head_dim)
    wave_length = 2.0 * math.pi / inverse
    smooth = (old_context / wave_length - low_factor) / (high_factor - low_factor)
    middle = (1.0 - smooth) * inverse / scale_factor + smooth * inverse
    scaled = jnp.where(wave_length > old_context / low_factor, inverse / scale_factor, inverse)
    inside = (wave_length >= old_context / high_factor) & (wave_length <= old_context / low_factor)
    return jnp.where(inside, middle, scaled)


def rotate(tensor, position):
    head_dim = tensor.shape[-1]
    half_size = head_dim // 2
    angles = position.astype(jnp.float32)[:, None] * frequencies(head_dim)[None, :]
    cosine = jnp.cos(angles)[:, None, :]
    sine_part = jnp.sin(angles)[:, None, :]
    widened = tensor.astype(jnp.float32)
    front_half = widened[..., :half_size]
    back_half = widened[..., half_size:]
    turned = jnp.concatenate(
        [front_half * cosine - back_half * sine_part, back_half * cosine + front_half * sine_part],
        axis=-1,
    )
    return turned.astype(jnp.bfloat16)


def key_mask(row_count, anchor_rows, length, anchor_live):
    query_index = jnp.arange(row_count, dtype=jnp.int32)[:, None]
    column = jnp.arange(anchor_rows + row_count, dtype=jnp.int32)[None, :]
    local_index = column - anchor_rows
    nearby = (local_index <= query_index) & (local_index < length)
    return jnp.where(column < anchor_rows, anchor_live, nearby)


def body(queries, keys, values, lengths):
    row_count = queries.shape[0]
    head_count = queries.shape[1] // HD
    group_count = keys.shape[1] // HD
    group_size = head_count // group_count
    score_scale = HD ** (-0.5)
    every_length = lax.all_gather(lengths, "ctx", axis=0, tiled=True)
    lower_ones = jnp.arange(every_length.shape[0], dtype=jnp.int32) < lax.axis_index("ctx")
    offset = jnp.sum(jnp.where(lower_ones, every_length, 0))
    length = lengths[0]
    position = offset + jnp.arange(row_count, dtype=jnp.int32)
    roped_queries = rotate(queries.reshape(row_count, head_count, HD), position)
    roped_keys = rotate(keys.reshape(row_count, group_count, HD), position).reshape(
        row_count, group_count * HD
    )
    anchor_rows = ANCHOR
    allowed = key_mask(row_count, anchor_rows, length, lax.axis_index("ctx") > 0)
    query_groups = roped_queries.reshape(row_count, group_count, group_size, HD).transpose(
        1, 2, 0, 3
    )

    def soften(scores):
        highest = jnp.max(scores, axis=-1, keepdims=True)
        raised = jnp.exp(scores - highest)
        return (raised.astype(jnp.bfloat16), jnp.sum(raised, axis=-1))

    def weigh_group(inputs):
        query_one, key_one = inputs
        scores = (
            jnp.einsum("pqd,kd->pqk", query_one, key_one, preferred_element_type=jnp.float32)
            * score_scale
        )
        scores = jnp.where(allowed[None], scores, masked_score)
        return soften(scores)

    def mix_group(inputs):
        weight_one, total_one, value_one = inputs
        mixed_one = jnp.einsum(
            "pqk,kd->pqd", weight_one, value_one, preferred_element_type=jnp.float32
        )
        return mixed_one / total_one[..., None]

    def split_heads(part_rows):
        return part_rows.reshape(part_rows.shape[0], group_count, HD).transpose(1, 0, 2)

    def stacked(anchor_part, own_part):
        return split_heads(jnp.concatenate([anchor_part, own_part], axis=0))

    anchor_keys, anchor_values = (spread(roped_keys, "ctx", 0), spread(values, "ctx", 0))
    weights, totals = lax.map(weigh_group, (query_groups, stacked(anchor_keys, roped_keys)))
    mixed_heads = lax.map(mix_group, (weights, totals, stacked(anchor_values, values)))
    live_rows = (jnp.arange(row_count, dtype=jnp.int32) < length)[:, None, None, None]
    output = jnp.where(live_rows, mixed_heads.transpose(2, 0, 1, 3), 0.0)
    return output.reshape(row_count, head_count * HD).astype(jnp.bfloat16)


def solution(mesh):
    return jax.shard_map(
        body,
        mesh=mesh,
        in_specs=(
            P(("grp", "ctx"), None),
            P(("grp", "ctx"), None),
            P(("grp", "ctx"), None),
            P(("grp", "ctx")),
        ),
        out_specs=P(("grp", "ctx"), None),
        check_vma=False,
    )
```

profile of v0, /device:TPU:0, one launch (start us, length us, event | category | flops | bytes accessed | tf_op | source)
XLA Modules:
  0.0 241.1 jit_solution(4858381081785082136)
XLA Ops:
  9.2 13.8 %all-reduce = s32[16]{0:T(128)S(1)} all-reduce(s32[16]{0:T(128)S(1)} %dynamic-update-slice), channel_id=1, replica_groups=mesh['grp'=2,'ctx'=16] {'ctx'}, use_global_device_ids=true, to_apply=%add | all-reduce | flops 16 | bytes 128
  29.4 3.2 %convert_bitcast_fusion = f32[32,8,64,128]{3,1,2,0:T(8,128)S(1)} fusion(bf16[256,8192]{1,0:T(8,128)(2,1)} %param.8), kind=kLoop, calls=%fused_computation.31 | loop fusion | flops 2097152 | bytes 12582912
  34.2 5.5 %fusion.34 = (f32[256,64,64]{2,1,0:T(8,128)S(1)}, f32[256,64,64]{2,1,0:T(8,128)}) fusion(f32[256,64,128]{2,1,0:T(8,128)S(1)} %bitcast.81), kind=kLoop, calls=%fused_computation.56 | loop fusion | bytes 16777216 | tf_op jit(solution)/shard_map/slice | solution.py:43
  39.7 11.7 %subtract_convert_fusion = (bf16[256,64,64]{2,0,1:T(8,128)(2,1)S(1)}, bf16[256,64,64]{2,0,1:T(8,128)(2,1)S(1)}) fusion(f32[256,64,64]{2,1,0:T(8,128)} %get-tuple-element.143, f32[256,64,64]{2,1,0:T(8,128)S(1)} %get-tuple-element.142, f32[256,64]{1,0:T(8,128)S(1)} %copy.11, f32[256,64]{1,0:T(8,128)S(1)} %copy.9), kind=kLoop, calls=%fused_computation.34 | loop fusion | flops 8388608 | bytes 12713984 | tf_op jit(solution)/shard_map/convert.5
  51.5 3.6 %maximum_bitcast_fusion = bf16[8,8,256,128]{3,2,1,0:T(8,128)(2,1)} fusion(bf16[256,8,8,64]{3,0,2,1:T(8,128)(2,1)S(1)} %bitcast.83, bf16[256,8,8,64]{3,0,2,1:T(8,128)(2,1)S(1)} %bitcast.82), kind=kLoop, calls=%fused_computation.37 | loop fusion | flops 8388608 | bytes 8388608 | tf_op jit(solution)/shard_map/transpose | solution.py:77
  55.1 65.6 %all-reduce.4.cloned.1.call-done = (bf16[256,8,128]{0,2,1:T(8,128)(2,1)}, bf16[256,1024]{0,1:T(8,128)(2,1)}) async-done(((bf16[256,8,128]{0,2,1:T(8,128)(2,1)}, bf16[256,1024]{0,1:T(8,128)(2,1)}), (bf16[256,8,128]{0,2,1:T(8,128)(2,1)}, bf16[256,1024]{0,1:T(8,128)(2,1)})) %all-reduce.4.cloned.1.call-update) | async-done | bytes 1048592 | tf_op jit(solution)/shard_map/psum | solution.py:22
  121.8 71.2 %while.26 = (s32[]{:T(128)}, bf16[8,8,256,512]{3,2,1,0:T(8,128)(2,1)}, f32[8,8,256]{2,1,0:T(8,128)S(1)}, bf16[8,8,256,128]{3,2,1,0:T(8,128)(2,1)}, bf16[8,512,12...) while((s32[]{:T(128)}, ...), condition=%wide.region_5.6_spmd.clone.clone, body=%wide.region_2.5_spmd.clone.sunk.clone | while | flops 276169216 | bytes 24146532 | solution.py:109
  123.8 4.5 %bitcast_dynamic-update-slice_fusion.6 = (bf16[8,8,256,512]{3,2,1,0:T(8,128)(2,1)}, f32[8,256,512]{2,1,0:T(8,128)}) fusion(bf16[8,8,256,512]{3,2,1,0:T(8,128)(2,1)} %get-tuple-element.283, s32[]{:T(128)} %get-tuple-element.282, f32[8,256,512]{2,1,0:T(8,128)S(1)} %fusion.54, pred[256,512]{1,0:T(8,128)(4,1)S(1)} %fusion.55), kind=kOutput, calls=%fused_computation.15.clone.1.clone | output fusion | flops 6294015 | bytes 14942720 | tf_op jit(solution)/shard_map/while/body/eval_jaxpr/sub | solution.py:83
  132.7 4.4 %bitcast_dynamic-update-slice_fusion.6 = (bf16[8,8,256,512]{3,2,1,0:T(8,128)(2,1)}, f32[8,256,512]{2,1,0:T(8,128)}) fusion(bf16[8,8,256,512]{3,2,1,0:T(8,128)(2,1)} %get-tuple-element.283, s32[]{:T(128)} %get-tuple-element.282, f32[8,256,512]{2,1,0:T(8,128)S(1)} %fusion.54, pred[256,512]{1,0:T(8,128)(4,1)S(1)} %fusion.55), kind=kOutput, calls=%fused_computation.15.clone.1.clone | output fusion | flops 6294015 | bytes 14942720 | tf_op jit(solution)/shard_map/while/body/eval_jaxpr/sub | solution.py:83
  141.5 4.4 %bitcast_dynamic-update-slice_fusion.6 = (bf16[8,8,256,512]{3,2,1,0:T(8,128)(2,1)}, f32[8,256,512]{2,1,0:T(8,128)}) fusion(bf16[8,8,256,512]{3,2,1,0:T(8,128)(2,1)} %get-tuple-element.283, s32[]{:T(128)} %get-tuple-element.282, f32[8,256,512]{2,1,0:T(8,128)S(1)} %fusion.54, pred[256,512]{1,0:T(8,128)(4,1)S(1)} %fusion.55), kind=kOutput, calls=%fused_computation.15.clone.1.clone | output fusion | flops 6294015 | bytes 14942720 | tf_op jit(solution)/shard_map/while/body/eval_jaxpr/sub | solution.py:83
  150.3 4.5 %bitcast_dynamic-update-slice_fusion.6 = (bf16[8,8,256,512]{3,2,1,0:T(8,128)(2,1)}, f32[8,256,512]{2,1,0:T(8,128)}) fusion(bf16[8,8,256,512]{3,2,1,0:T(8,128)(2,1)} %get-tuple-element.283, s32[]{:T(128)} %get-tuple-element.282, f32[8,256,512]{2,1,0:T(8,128)S(1)} %fusion.54, pred[256,512]{1,0:T(8,128)(4,1)S(1)} %fusion.55), kind=kOutput, calls=%fused_computation.15.clone.1.clone | output fusion | flops 6294015 | bytes 14942720 | tf_op jit(solution)/shard_map/while/body/eval_jaxpr/sub | solution.py:83
  159.3 4.5 %bitcast_dynamic-update-slice_fusion.6 = (bf16[8,8,256,512]{3,2,1,0:T(8,128)(2,1)}, f32[8,256,512]{2,1,0:T(8,128)}) fusion(bf16[8,8,256,512]{3,2,1,0:T(8,128)(2,1)} %get-tuple-element.283, s32[]{:T(128)} %get-tuple-element.282, f32[8,256,512]{2,1,0:T(8,128)S(1)} %fusion.54, pred[256,512]{1,0:T(8,128)(4,1)S(1)} %fusion.55), kind=kOutput, calls=%fused_computation.15.clone.1.clone | output fusion | flops 6294015 | bytes 14942720 | tf_op jit(solution)/shard_map/while/body/eval_jaxpr/sub | solution.py:83
  168.2 4.5 %bitcast_dynamic-update-slice_fusion.6 = (bf16[8,8,256,512]{3,2,1,0:T(8,128)(2,1)}, f32[8,256,512]{2,1,0:T(8,128)}) fusion(bf16[8,8,256,512]{3,2,1,0:T(8,128)(2,1)} %get-tuple-element.283, s32[]{:T(128)} %get-tuple-element.282, f32[8,256,512]{2,1,0:T(8,128)S(1)} %fusion.54, pred[256,512]{1,0:T(8,128)(4,1)S(1)} %fusion.55), kind=kOutput, calls=%fused_computation.15.clone.1.clone | output fusion | flops 6294015 | bytes 14942720 | tf_op jit(solution)/shard_map/while/body/eval_jaxpr/sub | solution.py:83
  177.1 4.5 %bitcast_dynamic-update-slice_fusion.6 = (bf16[8,8,256,512]{3,2,1,0:T(8,128)(2,1)}, f32[8,256,512]{2,1,0:T(8,128)}) fusion(bf16[8,8,256,512]{3,2,1,0:T(8,128)(2,1)} %get-tuple-element.283, s32[]{:T(128)} %get-tuple-element.282, f32[8,256,512]{2,1,0:T(8,128)S(1)} %fusion.54, pred[256,512]{1,0:T(8,128)(4,1)S(1)} %fusion.55), kind=kOutput, calls=%fused_computation.15.clone.1.clone | output fusion | flops 6294015 | bytes 14942720 | tf_op jit(solution)/shard_map/while/body/eval_jaxpr/sub | solution.py:83
  186.0 4.4 %bitcast_dynamic-update-slice_fusion.6 = (bf16[8,8,256,512]{3,2,1,0:T(8,128)(2,1)}, f32[8,256,512]{2,1,0:T(8,128)}) fusion(bf16[8,8,256,512]{3,2,1,0:T(8,128)(2,1)} %get-tuple-element.283, s32[]{:T(128)} %get-tuple-element.282, f32[8,256,512]{2,1,0:T(8,128)S(1)} %fusion.54, pred[256,512]{1,0:T(8,128)(4,1)S(1)} %fusion.55), kind=kOutput, calls=%fused_computation.15.clone.1.clone | output fusion | flops 6294015 | bytes 14942720 | tf_op jit(solution)/shard_map/while/body/eval_jaxpr/sub | solution.py:83
  193.1 24.8 %while.25 = (s32[]{:T(128)}, bf16[8,8,256,128]{3,2,1,0:T(8,128)(2,1)}, bf16[8,8,256,512]{3,2,1,0:T(8,128)(2,1)}, bf16[8,512,128]{1,2,0:T(8,128)(2,1)S(1)}, f32[8,8,256]{2,1,0:T(8,128)S(1)}) while((s32[]{:T(128)}, bf16[8,8,256,128]{3,2,1,0:T(8,128)(2,1)}, bf16[8,8,256,512]{3,2,1,0:T(8,128)(2,1)}, ...), condition=%wide.region_8.9_spmd.clone, body=%wide.region_7.8_spmd.sunk.clone | while | flops 268697600 | bytes 3302977 | solution.py:110
  193.1 3.1 %fusion.51 = bf16[8,8,256,128]{3,2,1,0:T(8,128)(2,1)} fusion(bf16[8,8,256,128]{3,2,1,0:T(8,128)(2,1)} %get-tuple-element.306, s32[]{:T(128)} %get-tuple-element.305, bf16[8,8,256,512]{3,2,1,0:T(8,128)(2,1)} %get-tuple-element.312, f32[8,256]{1,0:T(8,128)S(1)} %dynamic-slice_bitcast_fusion.3, bf16[8,512,128]{1,2,0:T(8,128)(2,1)S(1)} %get-tuple-element.313), kind=kOutput, calls=%fused_computation.6.clone.1.clone | convolution fusion | flops 268697600 | bytes 3286528 | tf_op jit(solution)/shard_map/while/body/eval_jaxpr/pqk,kd->pqd/dot_general | solution.py:97
  196.2 3.1 %fusion.51 = bf16[8,8,256,128]{3,2,1,0:T(8,128)(2,1)} fusion(bf16[8,8,256,128]{3,2,1,0:T(8,128)(2,1)} %get-tuple-element.306, s32[]{:T(128)} %get-tuple-element.305, bf16[8,8,256,512]{3,2,1,0:T(8,128)(2,1)} %get-tuple-element.312, f32[8,256]{1,0:T(8,128)S(1)} %dynamic-slice_bitcast_fusion.3, bf16[8,512,128]{1,2,0:T(8,128)(2,1)S(1)} %get-tuple-element.313), kind=kOutput, calls=%fused_computation.6.clone.1.clone | convolution fusion | flops 268697600 | bytes 3286528 | tf_op jit(solution)/shard_map/while/body/eval_jaxpr/pqk,kd->pqd/dot_general | solution.py:97
  199.3 3.1 %fusion.51 = bf16[8,8,256,128]{3,2,1,0:T(8,128)(2,1)} fusion(bf16[8,8,256,128]{3,2,1,0:T(8,128)(2,1)} %get-tuple-element.306, s32[]{:T(128)} %get-tuple-element.305, bf16[8,8,256,512]{3,2,1,0:T(8,128)(2,1)} %get-tuple-element.312, f32[8,256]{1,0:T(8,128)S(1)} %dynamic-slice_bitcast_fusion.3, bf16[8,512,128]{1,2,0:T(8,128)(2,1)S(1)} %get-tuple-element.313), kind=kOutput, calls=%fused_computation.6.clone.1.clone | convolution fusion | flops 268697600 | bytes 3286528 | tf_op jit(solution)/shard_map/while/body/eval_jaxpr/pqk,kd->pqd/dot_general | solution.py:97
  202.4 3.1 %fusion.51 = bf16[8,8,256,128]{3,2,1,0:T(8,128)(2,1)} fusion(bf16[8,8,256,128]{3,2,1,0:T(8,128)(2,1)} %get-tuple-element.306, s32[]{:T(128)} %get-tuple-element.305, bf16[8,8,256,512]{3,2,1,0:T(8,128)(2,1)} %get-tuple-element.312, f32[8,256]{1,0:T(8,128)S(1)} %dynamic-slice_bitcast_fusion.3, bf16[8,512,128]{1,2,0:T(8,128)(2,1)S(1)} %get-tuple-element.313), kind=kOutput, calls=%fused_computation.6.clone.1.clone | convolution fusion | flops 268697600 | bytes 3286528 | tf_op jit(solution)/shard_map/while/body/eval_jaxpr/pqk,kd->pqd/dot_general | solution.py:97
  208.6 3.1 %fusion.51 = bf16[8,8,256,128]{3,2,1,0:T(8,128)(2,1)} fusion(bf16[8,8,256,128]{3,2,1,0:T(8,128)(2,1)} %get-tuple-element.306, s32[]{:T(128)} %get-tuple-element.305, bf16[8,8,256,512]{3,2,1,0:T(8,128)(2,1)} %get-tuple-element.312, f32[8,256]{1,0:T(8,128)S(1)} %dynamic-slice_bitcast_fusion.3, bf16[8,512,128]{1,2,0:T(8,128)(2,1)S(1)} %get-tuple-element.313), kind=kOutput, calls=%fused_computation.6.clone.1.clone | convolution fusion | flops 268697600 | bytes 3286528 | tf_op jit(solution)/shard_map/while/body/eval_jaxpr/pqk,kd->pqd/dot_general | solution.py:97
  214.8 3.1 %fusion.51 = bf16[8,8,256,128]{3,2,1,0:T(8,128)(2,1)} fusion(bf16[8,8,256,128]{3,2,1,0:T(8,128)(2,1)} %get-tuple-element.306, s32[]{:T(128)} %get-tuple-element.305, bf16[8,8,256,512]{3,2,1,0:T(8,128)(2,1)} %get-tuple-element.312, f32[8,256]{1,0:T(8,128)S(1)} %dynamic-slice_bitcast_fusion.3, bf16[8,512,128]{1,2,0:T(8,128)(2,1)S(1)} %get-tuple-element.313), kind=kOutput, calls=%fused_computation.6.clone.1.clone | convolution fusion | flops 268697600 | bytes 3286528 | tf_op jit(solution)/shard_map/while/body/eval_jaxpr/pqk,kd->pqd/dot_general | solution.py:97
  217.9 3.4 %fusion.32 = bf16[256,8,8,128]{3,0,2,1:T(8,128)(2,1)S(1)} fusion(bf16[8,8,256,128]{3,2,1,0:T(8,128)(2,1)} %get-tuple-element.67, pred[256]{0:T(512)(128)(4,1)S(1)} %iota_compare_fusion.2), kind=kLoop, calls=%fused_computation.35 | loop fusion | flops 2097152 | bytes 8388864 | tf_op jit(solution)/shard_map/convert_element_type | solution.py:113
  224.1 10.2 %copy.29 = bf16[32,8,64,128]{3,1,2,0:T(8,128)(2,1)} copy(bf16[32,8,64,128]{3,2,1,0:T(8,128)(2,1)S(1)} %bitcast.84) | data formatting | bytes 8388608
  (72 shorter events, 55.2 us)
Async XLA Ops:
  6.5 114.2 %all-reduce.4.cloned.1.call-start = ((), (), s32[]{:S(2)}) async-start(), calls=%async_computation | async-start | bytes 2097152 | tf_op jit(solution)/shard_map/psum | solution.py:22
  121.8 71.2 %copy-start = (bf16[256,1024]{0,1:T(8,128)(2,1)S(1)}, bf16[256,1024]{0,1:T(8,128)(2,1)}, u32[]{:S(2)}) copy-start(bf16[256,1024]{0,1:T(8,128)(2,1)} %get-tuple-element.135) | copy-start | bytes 1572868
Sparse Core Ops, SparseCore 0:
  29.3 91.3 all-reduce.3
where the time goes:
time: 242 us; the launch traced here: 241 us
  other arithmetic  83.6 us (35%)
  waiting for transfers between devices  65.6 us (27%)
  matrix products  38.7 us (16%)
  local copies, waits for them, and re-layouts  24.8 us (10%)
  between operations  14.2 us (6%)
  blocking collectives  13.8 us (6%)
    psum x1, waiting for transfers between devices, spread(): return lax.psum(block, axis)  65.6 us
    sub x8, other arithmetic, soften(): raised = jnp.exp(scores - highest)  35.7 us
    dot_general x8, matrix products, mix_group(): jnp.einsum('pqk,kd->pqd', weight_one, value_one, preferred_element_type=j...  24.8 us
    reduce_sum x8, other arithmetic, soften(): return (raised.astype(jnp.bfloat16), jnp.sum(raised, axis=-1))  20.3 us
    unnamed x9, local copies, waits for them, and re-layouts  16.3 us
    dot_general x8, matrix products, weigh_group(): jnp.einsum('pqd,kd->pqk', query_one, key_one, preferred_element_type=jnp....  13.9 us
    unnamed x1, blocking collectives  13.8 us
    another operation x1, other arithmetic  11.7 us
  transfers between devices with their start and end apart: 1, of which 1 were waited for; matrix products, arithmetic and copies ran while one was open for 11% of the time, Pallas kernels for 0%

commit v1 on v0

v1 whole, which is shorter than its diff:
```python
import functools
import math

import jax
import jax.numpy as jnp
from jax import lax
from jax.experimental import pallas as pl
from jax.experimental.pallas import tpu as pltpu
from jax.sharding import PartitionSpec as P

HD = 128
ANCHOR = 256
NT = (((1,), (1,)), ((), ()))

rope_base = 500000.0
old_context = 8192.0
scale_factor = 8.0
low_factor = 1.0
high_factor = 4.0
masked_score = -1e30


def frequencies(head_dim):
    half_size = head_dim // 2
    inverse = rope_base ** (-2.0 * jnp.arange(half_size, dtype=jnp.float32) / head_dim)
    wave_length = 2.0 * math.pi / inverse
    smooth = (old_context / wave_length - low_factor) / (high_factor - low_factor)
    middle = (1.0 - smooth) * inverse / scale_factor + smooth * inverse
    scaled = jnp.where(wave_length > old_context / low_factor, inverse / scale_factor, inverse)
    inside = (wave_length >= old_context / high_factor) & (wave_length <= old_context / low_factor)
    return jnp.where(inside, middle, scaled)


def tables(position):
    angles = position.astype(jnp.float32)[:, None] * frequencies(HD)[None, :]
    cosine, sine = jnp.cos(angles), jnp.sin(angles)
    return jnp.concatenate([cosine, cosine], 1), jnp.concatenate([-sine, sine], 1)


def halving(count):
    steps, d = [], count // 2
    while d >= 1:
        steps.append([(h, h + d) for h in range(0, count, 2 * d)])
        d //= 2
    return steps


def plan(n):
    depth = n // 4
    tree = halving(depth)
    last = len(tree)
    at = lambda z, y, c: z * 4 + y * 2 + c
    steps = []
    for s in range(last + 2):
        pairs = []
        if s < last:
            pairs += [(at(a, 0, 0), at(b, 0, 0)) for a, b in tree[s]]
        elif s == last:
            pairs += [(at(z, 0, 0), at(z, 1, 0)) for z in range(depth)]
        if s == 0:
            pairs += [(at(0, 0, 1), at(0, 1, 1))]
        elif s <= last:
            pairs += [(at(a, 1, 1), at(b, 1, 1)) for a, b in tree[s - 1]]
        else:
            pairs += [(at(z, 1, 1), at(z, 0, 1)) for z in range(1, depth)]
        steps.append(pairs)
    return steps


def exchange(n, mask):
    return [(i, i ^ mask) for i in range(n)]


def send(x, pairs):
    return lax.ppermute(x, "ctx", pairs)


def spread(chunks_a, chunks_b, n):
    source = lax.axis_index("ctx") == 0
    held = []
    for a, b in zip(chunks_a, chunks_b):
        got = send(jnp.where(source, b, jnp.zeros_like(b)), exchange(n, 1))
        held.append(jnp.where(source, a, got))
    for pairs in plan(n):
        got = [send(x, pairs) for x in held]
        held = [x + g for x, g in zip(held, got)]
    other = [send(x, exchange(n, 1)) for x in held]
    return held, other


def offset_of(length, n):
    me = lax.axis_index("ctx")
    before, total, mask = jnp.zeros_like(length), length, 1
    while mask < n:
        got = send(total, exchange(n, mask))
        before = before + jnp.where((me & mask) > 0, got, 0)
        total = total + got
        mask *= 2
    return before


def rope(x, c, s):
    x = x.astype(jnp.float32)
    return (x * c + pltpu.roll(x, HD // 2, 1) * s).astype(jnp.bfloat16)


def attend(info, q_ref, k_ref, v_ref, ka_ref, va_ref, kb_ref, vb_ref, c_ref, s_ref, ca_ref, sa_ref, *refs, gs, sub):
    o_ref, qs, kc, vc = refs[-4:]
    length, first, mine = info[0], info[1] > 0, info[2] > 0
    rows, anchor = q_ref.shape[0], ka_ref.shape[0]
    half = rows // 2
    c, s = c_ref[...], s_ref[...]
    kr = rope(k_ref[...], c, s)
    ka = jnp.where(mine, ka_ref[...].astype(jnp.float32), kb_ref[...].astype(jnp.float32))
    va = jnp.where(mine, va_ref[...].astype(jnp.float32), vb_ref[...].astype(jnp.float32))
    kar = rope(ka, ca_ref[...], sa_ref[...])
    copy0 = jnp.broadcast_to(kr[:1].astype(jnp.float32), (anchor, HD))
    kc[:anchor, :] = jnp.where(first, copy0, kar.astype(jnp.float32)).astype(jnp.bfloat16)
    kc[anchor:, :] = kr
    live = jnp.where(first, 0.0, 1.0).astype(jnp.float32)
    vc[:anchor, :HD] = jnp.where(first, 0.0, va).astype(jnp.bfloat16)
    vc[:anchor, HD:] = jnp.full((anchor, HD), live, jnp.float32).astype(jnp.bfloat16)
    vc[anchor:, :HD] = v_ref[...]
    vc[anchor:, HD:] = jnp.ones((rows, HD), jnp.bfloat16)
    for r in range(2):
        span = slice(r * half, (r + 1) * half)
        for h in range(gs):
            qs[r, h * half:(h + 1) * half, :] = rope(q_ref[span, h * HD:(h + 1) * HD], c[span], s[span])
    tri = lax.broadcasted_iota(jnp.int32, (half, half), 0) >= lax.broadcasted_iota(jnp.int32, (half, half), 1)
    factor = HD ** -0.5 * math.log2(math.e)
    for r in range(2):
        n = anchor + (r + 1) * half
        span = slice(r * half, (r + 1) * half)
        valid = lax.broadcasted_iota(jnp.int32, (half, HD), 0) + r * half < length
        for h0 in range(0, gs, sub):
            q = qs[r, h0 * half:(h0 + sub) * half, :]
            scores = lax.dot_general(q, kc[:n, :], NT, preferred_element_type=jnp.float32)
            diag = scores[:, n - half:].reshape(sub, half, half)
            diag = jnp.where(tri[None], diag, masked_score).reshape(sub * half, half)
            rest = scores[:, :n - half]
            top = diag
            for t in range(0, n - half, HD):
                top = jnp.maximum(top, rest[:, t:t + HD])
            top = jnp.max(top, axis=1, keepdims=True)
            weights = jnp.concatenate(
                [jnp.exp2((rest - top) * factor).astype(jnp.bfloat16), jnp.exp2((diag - top) * factor).astype(jnp.bfloat16)], axis=1)
            mixed = jnp.dot(weights, vc[:n, :], preferred_element_type=jnp.float32)
            for i in range(sub):
                part = mixed[i * half:(i + 1) * half]
                inv = jnp.where(valid, 1.0 / part[:, HD:], 0.0)
                o_ref[span, (h0 + i) * HD:(h0 + i + 1) * HD] = (part[:, :HD] * inv).astype(jnp.bfloat16)


def attention(info, q, k, v, held, other, own, anchors, old, start, sub=8):
    rows, anchor = q.shape[0], held.shape[0] // 2
    groups = held.shape[1] // HD
    gs = q.shape[1] // k.shape[1]
    col = lambda n, w: pl.BlockSpec((n, w), lambda g, *_: (0, g + start * groups))
    top = pl.BlockSpec((anchor, HD), lambda g, *_: (0, g))
    low = pl.BlockSpec((anchor, HD), lambda g, *_: (1, g))
    full = lambda n: pl.BlockSpec((n, HD), lambda g, *_: (0, 0))
    return pl.pallas_call(
        functools.partial(attend, gs=gs, sub=sub),
        out_shape=jax.ShapeDtypeStruct(q.shape, jnp.bfloat16),
        grid_spec=pltpu.PrefetchScalarGridSpec(
            num_scalar_prefetch=1, grid=(groups,),
            in_specs=[col(rows, gs * HD), col(rows, HD), col(rows, HD), top, low, top, low,
                      full(rows), full(rows), full(anchor), full(anchor)] + [pl.BlockSpec(memory_space=pl.ANY)] * len(old),
            out_specs=col(rows, gs * HD),
            scratch_shapes=[pltpu.VMEM((2, gs * rows // 2, HD), jnp.bfloat16),
                            pltpu.VMEM((anchor + rows, HD), jnp.bfloat16),
                            pltpu.VMEM((anchor + rows, 2 * HD), jnp.bfloat16)]),
        input_output_aliases={12: 0} if old else {},
        compiler_params=pltpu.CompilerParams(vmem_limit_bytes=60 << 20),
        name="attend",
    )(info, q, k, v, held, held, other, other, *own, *anchors, *old)


def body(n, queries, keys, values, lengths):
    rows, width = keys.shape
    streams = 2
    parts = 2 * streams
    w = width // parts
    me = lax.axis_index("ctx")
    own = [jnp.concatenate([keys[:ANCHOR, c * w:(c + 1) * w], values[:ANCHOR, c * w:(c + 1) * w]], 0) for c in range(parts)]
    held, other = spread(own[0::2], own[1::2], n)
    offset = offset_of(lengths, n)
    info = lambda mine: jnp.stack([lengths[0], (me == 0).astype(jnp.int32), mine.astype(jnp.int32)])
    mine_tab = tables(offset + jnp.arange(rows, dtype=jnp.int32))
    anchor_tab = tables(jnp.arange(ANCHOR, dtype=jnp.int32))
    old = ()
    for c in range(parts):
        mine = (me & 1) == (c & 1)
        old = (attention(info(mine), queries, keys, values, held[c // 2], other[c // 2], mine_tab, anchor_tab, old, c),)
    return old[0]


def solution(mesh):
    spec = P(("grp", "ctx"), None)
    return jax.shard_map(
        functools.partial(body, mesh.shape["ctx"]), mesh=mesh,
        in_specs=(spec, spec, spec, P(("grp", "ctx"))), out_specs=spec, check_vma=False)
```

time: 242 us -> 76.5 us (0.32)
  other arithmetic: 83.6 us -> 4.71 us
  waiting for transfers between devices: 65.6 us -> 9.51 us
  matrix products: 38.7 us -> 0 us
  starting transfers between devices: 0.01 us -> 27.1 us
  Pallas kernels: 0 us -> 26.6 us
  local copies, waits for them, and re-layouts: 24.8 us -> 2.75 us
  blocking collectives: 13.8 us -> 0 us
  between operations: 14.2 us -> 5.33 us
    psum x1 -> x0, waiting for transfers between devices: 65.6 us -> none  [spread(): return lax.psum(block, axis)]
    dot_general x16 -> x0, matrix products: 38.7 us -> none  [the longest x8 24.8 us: mix_group(): jnp.einsum('pqk,kd->pqd', weight_one, value_one, preferred_element_type=j...]
    sub x10 -> x0, other arithmetic: 35.8 us -> none  [the longest x8 35.7 us: soften(): raised = jnp.exp(scores - highest)]
    ppermute x0 -> x16, starting transfers between devices: none -> 27.1 us  [send(): return lax.ppermute(x, 'ctx', pairs)]
    pallas_call x0 -> x4, Pallas kernels: none -> 26.6 us  [attention(): pl.pallas_call(functools.partial(attend, gs=gs, sub=sub), out_shape=jax.S...]
    reduce_sum x9 -> x0, other arithmetic: 20.9 us -> none  [the longest x8 20.3 us: soften(): return (raised.astype(jnp.bfloat16), jnp.sum(raised, axis=-1))]
    unnamed x9 -> x8, local copies, waits for them, and re-layouts: 16.3 us -> 1.39 us
    unnamed x1 -> x0, blocking collectives: 13.8 us -> none
  transfers between devices with their start and end apart: 1 -> 16, of which waited for: 1 -> 6; matrix products, arithmetic and copies ran while one was open for 11% -> 6% of each run, Pallas kernels for 0% -> 17%
where the time goes in v1:
time: 76.5 us; the launch traced here: 76 us
  starting transfers between devices  27.1 us (35%)
  Pallas kernels  26.6 us (35%)
  waiting for transfers between devices  9.51 us (12%)
  between operations  5.33 us (7%)
  other arithmetic  4.71 us (6%)
  local copies, waits for them, and re-layouts  2.75 us (4%)
    ppermute x16, starting transfers between devices, send(): return lax.ppermute(x, 'ctx', pairs)  27.1 us
    pallas_call x4, Pallas kernels, attention(): pl.pallas_call(functools.partial(attend, gs=gs, sub=sub), out_shape=jax.S...  26.6 us
    ppermute x16, waiting for transfers between devices, send(): return lax.ppermute(x, 'ctx', pairs)  9.51 us
    concatenate x2, other arithmetic, tables(): jnp.concatenate([cosine, cosine], 1)  1.67 us
  transfers between devices with their start and end apart: 16, of which 6 were waited for; matrix products, arithmetic and copies ran while one was open for 6% of the time, Pallas kernels for 17%

profile of v1, /device:TPU:0, one launch (start us, length us, event | category | flops | bytes accessed | tf_op | source)
XLA Modules:
  0.0 76.0 jit_solution(5282797720702586140)
XLA Ops:
  0.0 1.4 %fusion.2 = (bf16[256,256]{1,0:T(8,128)(2,1)S(1)}, bf16[256,256]{1,0:T(8,128)(2,1)S(1)}, bf16[256,256]{1,0:T(8,128)(2,1)S(1)}, bf16[256,256]{1,0:T(8,128)(2,1)S(...) fusion(bf16[256,1024]{1,0:T(8,128)(2,1)} %k_ref.7, ...), kind=kLoop, calls=%fused_computation.21 | loop fusion | bytes 2097152 | tf_op jit(solution)/shard_map/slice | solution.py:185
  2.1 1.0 %collective-permute-done = bf16[512,256]{1,0:T(8,128)(2,1)S(1)} collective-permute-done((bf16[512,256]{1,0:T(8,128)(2,1)S(1)}, bf16[512,256]{1,0:T(8,128)(2,1)S(1)}, u32[]{:S(2)}, u32[]{:S(2)}) %collective-permute-start) | collective-permute-done | bytes 262176 | tf_op jit(solution)/shard_map/ppermute | solution.py:75
  3.2 5.9 %collective-permute-start.1 = (bf16[512,256]{1,0:T(8,128)(2,1)S(1)}, bf16[512,256]{1,0:T(8,128)(2,1)S(1)}, u32[]{:S(2)}, u32[]{:S(2)}) collective-permute-start(bf16[512,256]{1,0:T(8,128)(2,1)S(1)} %maximum_select_fusion), channel_id=1, source_target_pairs={{0,8},{1,3},{16,24},{17,19}} | collective-permute-start | bytes 786440 | tf_op jit(solution)/shard_map/ppermute | solution.py:75
  9.2 1.3 %collective-permute-start.11 = (bf16[512,256]{1,0:T(8,128)(2,1)S(1)}, bf16[512,256]{1,0:T(8,128)(2,1)S(1)}, u32[]{:S(2)}, u32[]{:S(2)}) collective-permute-start(bf16[512,256]{1,0:T(8,128)(2,1)S(1)} %maximum_select_fusion.2), channel_id=1, source_target_pairs={{0,8},{1,3},{16,24},{17,19}} | collective-permute-start | bytes 786440 | tf_op jit(solution)/shard_map/ppermute | solution.py:75
  10.5 2.5 %collective-permute-done.1 = bf16[512,256]{1,0:T(8,128)(2,1)S(1)} collective-permute-done((bf16[512,256]{1,0:T(8,128)(2,1)S(1)}, bf16[512,256]{1,0:T(8,128)(2,1)S(1)}, u32[]{:S(2)}, u32[]{:S(2)}) %collective-permute-start.1) | collective-permute-done | bytes 262176 | tf_op jit(solution)/shard_map/ppermute | solution.py:75
  13.0 1.3 %collective-permute-start.2 = (bf16[512,256]{1,0:T(8,128)(2,1)S(1)}, bf16[512,256]{1,0:T(8,128)(2,1)S(1)}, u32[]{:S(2)}, u32[]{:S(2)}) collective-permute-start(bf16[512,256]{1,0:T(8,128)(2,1)S(1)} %add.77), channel_id=1, source_target_pairs={{0,4},{8,12},{3,11},{16,20},{24,28},{19,27}} | collective-permute-start | bytes 786440 | tf_op jit(solution)/shard_map/ppermute | solution.py:75
  14.3 1.4 %collective-permute-done.11 = bf16[512,256]{1,0:T(8,128)(2,1)S(1)} collective-permute-done((bf16[512,256]{1,0:T(8,128)(2,1)S(1)}, bf16[512,256]{1,0:T(8,128)(2,1)S(1)}, u32[]{:S(2)}, u32[]{:S(2)}) %collective-permute-start.11) | collective-permute-done | bytes 262176 | tf_op jit(solution)/shard_map/ppermute | solution.py:75
  15.8 1.3 %collective-permute-start.12 = (bf16[512,256]{1,0:T(8,128)(2,1)S(1)}, bf16[512,256]{1,0:T(8,128)(2,1)S(1)}, u32[]{:S(2)}, u32[]{:S(2)}) collective-permute-start(bf16[512,256]{1,0:T(8,128)(2,1)S(1)} %add.91), channel_id=1, source_target_pairs={{0,4},{8,12},{3,11},{16,20},{24,28},{19,27}} | collective-permute-start | bytes 786440 | tf_op jit(solution)/shard_map/ppermute | solution.py:75
  17.1 1.4 %collective-permute-done.2 = bf16[512,256]{1,0:T(8,128)(2,1)S(1)} collective-permute-done((bf16[512,256]{1,0:T(8,128)(2,1)S(1)}, bf16[512,256]{1,0:T(8,128)(2,1)S(1)}, u32[]{:S(2)}, u32[]{:S(2)}) %collective-permute-start.2) | collective-permute-done | bytes 262176 | tf_op jit(solution)/shard_map/ppermute | solution.py:75
  18.6 1.3 %collective-permute-start.3 = (bf16[512,256]{1,0:T(8,128)(2,1)S(1)}, bf16[512,256]{1,0:T(8,128)(2,1)S(1)}, u32[]{:S(2)}, u32[]{:S(2)}) collective-permute-start(bf16[512,256]{1,0:T(8,128)(2,1)S(1)} %add.78), channel_id=1, source_target_pairs={{0,2},{4,6},{8,10},{12,14},{3,7},{11,15},{16,18},{20,22},{24,26},{... | collective-permute-start | bytes 786440 | tf_op jit(solution)/shard_map/ppermute | solution.py:75
  19.9 1.4 %collective-permute-done.12 = bf16[512,256]{1,0:T(8,128)(2,1)S(1)} collective-permute-done((bf16[512,256]{1,0:T(8,128)(2,1)S(1)}, bf16[512,256]{1,0:T(8,128)(2,1)S(1)}, u32[]{:S(2)}, u32[]{:S(2)}) %collective-permute-start.12) | collective-permute-done | bytes 262176 | tf_op jit(solution)/shard_map/ppermute | solution.py:75
  21.4 1.3 %collective-permute-start.13 = (bf16[512,256]{1,0:T(8,128)(2,1)S(1)}, bf16[512,256]{1,0:T(8,128)(2,1)S(1)}, u32[]{:S(2)}, u32[]{:S(2)}) collective-permute-start(bf16[512,256]{1,0:T(8,128)(2,1)S(1)} %add.92), channel_id=1, source_target_pairs={{0,2},{4,6},{8,10},{12,14},{3,7},{11,15},{16,18},{20,22},{24,26},{... | collective-permute-start | bytes 786440 | tf_op jit(solution)/shard_map/ppermute | solution.py:75
  24.9 1.7 %collective-permute-done.13 = bf16[512,256]{1,0:T(8,128)(2,1)S(1)} collective-permute-done((bf16[512,256]{1,0:T(8,128)(2,1)S(1)}, bf16[512,256]{1,0:T(8,128)(2,1)S(1)}, u32[]{:S(2)}, u32[]{:S(2)}) %collective-permute-start.13) | collective-permute-done | bytes 262176 | tf_op jit(solution)/shard_map/ppermute | solution.py:75
  28.7 3.8 %collective-permute-start.7 = (s32[1]{0:T(128)}, s32[1]{0:T(128)}, u32[]{:S(2)}, u32[]{:S(2)}) collective-permute-start(s32[1]{0:T(128)} %add.81), channel_id=1, source_target_pairs={{0,2},{1,3},{2,0},{3,1},{4,6},{5,7},{6,4},{7,5},{8,10},{9,11},{10,... | collective-permute-start | bytes 20 | tf_op jit(solution)/shard_map/ppermute | solution.py:75
  33.8 3.8 %collective-permute-start.8 = (s32[1]{0:T(128)}, s32[1]{0:T(128)}, u32[]{:S(2)}, u32[]{:S(2)}) collective-permute-start(s32[1]{0:T(128)} %add.83), channel_id=1, source_target_pairs={{0,4},{1,5},{2,6},{3,7},{4,0},{5,1},{6,2},{7,3},{8,12},{9,13},{10,... | collective-permute-start | bytes 20 | tf_op jit(solution)/shard_map/ppermute | solution.py:75
  39.0 4.4 %collective-permute-start.9 = (s32[1]{0:T(128)}, s32[1]{0:T(128)}, u32[]{:S(2)}, u32[]{:S(2)}) collective-permute-start(s32[1]{0:T(128)} %add.85), channel_id=1, source_target_pairs={{0,8},{1,9},{2,10},{3,11},{4,12},{5,13},{6,14},{7,15},{8,0},{9,1},... | collective-permute-start | bytes 20 | tf_op jit(solution)/shard_map/ppermute | solution.py:75
  45.4 1.0 %fusion.1 = (f32[256,64]{1,0:T(8,128)S(1)}, f32[256,64]{1,0:T(8,128)S(1)}, f32[256,64]{1,0:T(8,128)S(1)}, f32[256,64]{1,0:T(8,128)S(1)}, f32[256,64]{1,0:T(8,128)S(1)}, /*index=5*/f32[256,64]{1,0:T(8,128)S(1)}) fusion(f32[64]{0:T(128)S(1)} %and_select_fusion, f32[256]{0:T(256)S(1)} %iota_convert_fusion, f32[256]{0:T(256)S(1)} %add_convert_fusion), kind=kLoop, calls=%fused_computation.13 | loop fusion | flops 65536 | bytes 395520 | tf_op jit(solution)/shard_map/neg | solution.py:37
  46.4 0.8 %pad_maximum_fusion.2 = (f32[256,128]{1,0:T(8,128)}, f32[256,128]{1,0:T(8,128)}) fusion(f32[256,64]{1,0:T(8,128)S(1)} %get-tuple-element.14, f32[256,64]{1,0:T(8,128)S(1)} %get-tuple-element.15, f32[256,64]{1,0:T(8,128)S(1)} %get-tuple-element.13), kind=kLoop, calls=%fused_computation.10 | loop fusion | flops 65536 | bytes 458752 | tf_op jit(solution)/shard_map/concatenate | solution.py:37
  47.2 0.8 %pad_maximum_fusion = (f32[256,128]{1,0:T(8,128)}, f32[256,128]{1,0:T(8,128)}) fusion(f32[256,64]{1,0:T(8,128)S(1)} %get-tuple-element.19, f32[256,64]{1,0:T(8,128)S(1)} %get-tuple-element.20, f32[256,64]{1,0:T(8,128)S(1)} %get-tuple-element.21), kind=kLoop, calls=%fused_computation.8 | loop fusion | flops 65536 | bytes 458752 | tf_op jit(solution)/shard_map/concatenate | solution.py:37
  48.7 6.6 %attend.4.refs_0_ = bf16[256,8192]{1,0:T(8,128)(2,1)} custom-call(s32[3]{0:T(128)} %pad_add_fusion.2.info, bf16[256,8192]{1,0:T(8,128)(2,1)} %q_ref.7, bf16[256,1024]{1,0:T(8,128)(2,1)} %k_ref.7, bf16[256,1024]{1,0:T(8,128)(2,1)} %v_ref.7, bf16[512,256]{1,0:T(8,128)(2,1)} %copy-done.1, bf16[512,256]{1,0:T(8,128)(2,1)} %copy-done.1, ...), custom_call_target="tpu_custom_call" | custom-call | tf_op jit(solution)/shard_map/attend/pallas_call | solution.py:162
  55.4 6.7 %attend.5.refs_0_ = bf16[256,8192]{1,0:T(8,128)(2,1)} custom-call(s32[3]{0:T(128)} %pad_add_fusion.info, bf16[256,8192]{1,0:T(8,128)(2,1)} %q_ref.7, bf16[256,1024]{1,0:T(8,128)(2,1)} %k_ref.7, bf16[256,1024]{1,0:T(8,128)(2,1)} %v_ref.7, bf16[512,256]{1,0:T(8,128)(2,1)} %copy-done.1, bf16[512,256]{1,0:T(8,128)(2,1)} %copy-done.1, ...), custom_call_target="tpu_custom_call", output_to_operand_aliasing={{}: (12, {})} | custom-call | tf_op jit(solution)/shard_map/attend/pallas_call | solution.py:162
  62.0 0.7 copy-done.2
  62.7 6.6 %attend.6.refs_0_ = bf16[256,8192]{1,0:T(8,128)(2,1)} custom-call(s32[3]{0:T(128)} %pad_add_fusion.2.info, bf16[256,8192]{1,0:T(8,128)(2,1)} %q_ref.7, bf16[256,1024]{1,0:T(8,128)(2,1)} %k_ref.7, bf16[256,1024]{1,0:T(8,128)(2,1)} %v_ref.7, bf16[512,256]{1,0:T(8,128)(2,1)} %copy-done, bf16[512,256]{1,0:T(8,128)(2,1)} %copy-done, ...), custom_call_target="tpu_custom_call", output_to_operand_aliasing={{}: (12, {})} | custom-call | tf_op jit(solution)/shard_map/attend/pallas_call | solution.py:162
  69.3 6.6 %attend.7 = bf16[256,8192]{1,0:T(8,128)(2,1)} custom-call(s32[3]{0:T(128)} %pad_add_fusion.info, bf16[256,8192]{1,0:T(8,128)(2,1)} %q_ref.7, bf16[256,1024]{1,0:T(8,128)(2,1)} %k_ref.7, bf16[256,1024]{1,0:T(8,128)(2,1)} %v_ref.7, bf16[512,256]{1,0:T(8,128)(2,1)} %copy-done, bf16[512,256]{1,0:T(8,128)(2,1)} %copy-done, ...), custom_call_target="tpu_custom_call", output_to_operand_aliasing={{}: (12, {})} | custom-call | tf_op jit(solution)/shard_map/attend/pallas_call | solution.py:162
  (41 shorter events, 5.5 us)
Async XLA Ops:
  1.4 1.7 %collective-permute-start = (bf16[512,256]{1,0:T(8,128)(2,1)S(1)}, bf16[512,256]{1,0:T(8,128)(2,1)S(1)}, u32[]{:S(2)}, u32[]{:S(2)}) collective-permute-start(bf16[512,256]{1,0:T(8,128)(2,1)S(1)} %maximum_select_fusion.1), channel_id=1, source_target_pairs={{0,1},{1,0},{2,3},{3,2},{4,5},{5,4},{6,7},{7,6},{8,9},{9,8},{10,11... | collective-permute-start | bytes 786440 | tf_op jit(solution)/shard_map/ppermute | solution.py:75
  2.0 7.1 %collective-permute-start.10 = (bf16[512,256]{1,0:T(8,128)(2,1)S(1)}, bf16[512,256]{1,0:T(8,128)(2,1)S(1)}, u32[]{:S(2)}, u32[]{:S(2)}) collective-permute-start(bf16[512,256]{1,0:T(8,128)(2,1)S(1)} %maximum_select_fusion.3), channel_id=1, source_target_pairs={{0,1},{1,0},{2,3},{3,2},{4,5},{5,4},{6,7},{7,6},{8,9},{9,8},{10,11... | collective-permute-start | bytes 786440 | tf_op jit(solution)/shard_map/ppermute | solution.py:75
  3.2 9.7 %collective-permute-start.1 = (bf16[512,256]{1,0:T(8,128)(2,1)S(1)}, bf16[512,256]{1,0:T(8,128)(2,1)S(1)}, u32[]{:S(2)}, u32[]{:S(2)}) collective-permute-start(bf16[512,256]{1,0:T(8,128)(2,1)S(1)} %maximum_select_fusion), channel_id=1, source_target_pairs={{0,8},{1,3},{16,24},{17,19}} | collective-permute-start | bytes 786440 | tf_op jit(solution)/shard_map/ppermute | solution.py:75
  9.2 6.6 %collective-permute-start.11 = (bf16[512,256]{1,0:T(8,128)(2,1)S(1)}, bf16[512,256]{1,0:T(8,128)(2,1)S(1)}, u32[]{:S(2)}, u32[]{:S(2)}) collective-permute-start(bf16[512,256]{1,0:T(8,128)(2,1)S(1)} %maximum_select_fusion.2), channel_id=1, source_target_pairs={{0,8},{1,3},{16,24},{17,19}} | collective-permute-start | bytes 786440 | tf_op jit(solution)/shard_map/ppermute | solution.py:75
  13.0 5.5 %collective-permute-start.2 = (bf16[512,256]{1,0:T(8,128)(2,1)S(1)}, bf16[512,256]{1,0:T(8,128)(2,1)S(1)}, u32[]{:S(2)}, u32[]{:S(2)}) collective-permute-start(bf16[512,256]{1,0:T(8,128)(2,1)S(1)} %add.77), channel_id=1, source_target_pairs={{0,4},{8,12},{3,11},{16,20},{24,28},{19,27}} | collective-permute-start | bytes 786440 | tf_op jit(solution)/shard_map/ppermute | solution.py:75
  15.8 5.5 %collective-permute-start.12 = (bf16[512,256]{1,0:T(8,128)(2,1)S(1)}, bf16[512,256]{1,0:T(8,128)(2,1)S(1)}, u32[]{:S(2)}, u32[]{:S(2)}) collective-permute-start(bf16[512,256]{1,0:T(8,128)(2,1)S(1)} %add.91), channel_id=1, source_target_pairs={{0,4},{8,12},{3,11},{16,20},{24,28},{19,27}} | collective-permute-start | bytes 786440 | tf_op jit(solution)/shard_map/ppermute | solution.py:75
  18.6 5.5 %collective-permute-start.3 = (bf16[512,256]{1,0:T(8,128)(2,1)S(1)}, bf16[512,256]{1,0:T(8,128)(2,1)S(1)}, u32[]{:S(2)}, u32[]{:S(2)}) collective-permute-start(bf16[512,256]{1,0:T(8,128)(2,1)S(1)} %add.78), channel_id=1, source_target_pairs={{0,2},{4,6},{8,10},{12,14},{3,7},{11,15},{16,18},{20,22},{24,26},{... | collective-permute-start | bytes 786440 | tf_op jit(solution)/shard_map/ppermute | solution.py:75
  21.4 5.2 %collective-permute-start.13 = (bf16[512,256]{1,0:T(8,128)(2,1)S(1)}, bf16[512,256]{1,0:T(8,128)(2,1)S(1)}, u32[]{:S(2)}, u32[]{:S(2)}) collective-permute-start(bf16[512,256]{1,0:T(8,128)(2,1)S(1)} %add.92), channel_id=1, source_target_pairs={{0,2},{4,6},{8,10},{12,14},{3,7},{11,15},{16,18},{20,22},{24,26},{... | collective-permute-start | bytes 786440 | tf_op jit(solution)/shard_map/ppermute | solution.py:75
  22.7 5.3 %collective-permute-start.6 = (s32[1]{0:T(128)}, s32[1]{0:T(128)}, u32[]{:S(2)}, u32[]{:S(2)}) collective-permute-start(s32[1]{0:T(128)} %param.7), channel_id=1, source_target_pairs={{0,1},{1,0},{2,3},{3,2},{4,5},{5,4},{6,7},{7,6},{8,9},{9,8},{10,11... | collective-permute-start | bytes 20 | tf_op jit(solution)/shard_map/ppermute | solution.py:75
  24.2 20.3 %collective-permute-start.4 = (bf16[512,256]{1,0:T(8,128)(2,1)S(1)}, bf16[512,256]{1,0:T(8,128)(2,1)S(1)}, u32[]{:S(2)}, u32[]{:S(2)}) collective-permute-start(bf16[512,256]{1,0:T(8,128)(2,1)S(1)} %add.79), channel_id=1, source_target_pairs={{7,5},{11,9},{15,13},{23,21},{27,25},{31,29}} | collective-permute-start | bytes 786440 | tf_op jit(solution)/shard_map/ppermute | solution.py:75
  26.7 18.0 %collective-permute-start.14 = (bf16[512,256]{1,0:T(8,128)(2,1)S(1)}, bf16[512,256]{1,0:T(8,128)(2,1)S(1)}, u32[]{:S(2)}, u32[]{:S(2)}) collective-permute-start(bf16[512,256]{1,0:T(8,128)(2,1)S(1)} %add.93), channel_id=1, source_target_pairs={{7,5},{11,9},{15,13},{23,21},{27,25},{31,29}} | collective-permute-start | bytes 786440 | tf_op jit(solution)/shard_map/ppermute | solution.py:75
  28.7 4.5 %collective-permute-start.7 = (s32[1]{0:T(128)}, s32[1]{0:T(128)}, u32[]{:S(2)}, u32[]{:S(2)}) collective-permute-start(s32[1]{0:T(128)} %add.81), channel_id=1, source_target_pairs={{0,2},{1,3},{2,0},{3,1},{4,6},{5,7},{6,4},{7,5},{8,10},{9,11},{10,... | collective-permute-start | bytes 20 | tf_op jit(solution)/shard_map/ppermute | solution.py:75
  33.8 4.5 %collective-permute-start.8 = (s32[1]{0:T(128)}, s32[1]{0:T(128)}, u32[]{:S(2)}, u32[]{:S(2)}) collective-permute-start(s32[1]{0:T(128)} %add.83), channel_id=1, source_target_pairs={{0,4},{1,5},{2,6},{3,7},{4,0},{5,1},{6,2},{7,3},{8,12},{9,13},{10,... | collective-permute-start | bytes 20 | tf_op jit(solution)/shard_map/ppermute | solution.py:75
  39.0 5.0 %collective-permute-start.9 = (s32[1]{0:T(128)}, s32[1]{0:T(128)}, u32[]{:S(2)}, u32[]{:S(2)}) collective-permute-start(s32[1]{0:T(128)} %add.85), channel_id=1, source_target_pairs={{0,8},{1,9},{2,10},{3,11},{4,12},{5,13},{6,14},{7,15},{8,0},{9,1},... | collective-permute-start | bytes 20 | tf_op jit(solution)/shard_map/ppermute | solution.py:75
  44.6 10.7 %copy-start = (bf16[512,256]{1,0:T(8,128)(2,1)}, bf16[512,256]{1,0:T(8,128)(2,1)S(1)}, u32[]{:S(2)}) copy-start(bf16[512,256]{1,0:T(8,128)(2,1)S(1)} %add.80.ka_ref.va_ref) | copy-start | bytes 786436
  44.6 17.4 %collective-permute-start.5 = (bf16[512,256]{1,0:T(8,128)(2,1)S(1)}, bf16[512,256]{1,0:T(8,128)(2,1)S(1)}, u32[]{:S(2)}, u32[]{:S(2)}) collective-permute-start(bf16[512,256]{1,0:T(8,128)(2,1)S(1)} %add.80.ka_ref.va_ref), channel_id=1, source_target_pairs={{0,1},{1,0},{2,3},{3,2},{4,5},{5,4},{6,7},{7,6},{8,9},{9,8},{10,11... | collective-permute-start | bytes 786440 | tf_op jit(solution)/shard_map/ppermute | solution.py:75
  44.8 3.2 %copy-start.1 = (bf16[512,256]{1,0:T(8,128)(2,1)}, bf16[512,256]{1,0:T(8,128)(2,1)S(1)}, u32[]{:S(2)}) copy-start(bf16[512,256]{1,0:T(8,128)(2,1)S(1)} %add.94.ka_ref.va_ref) | copy-start | bytes 786436
  44.8 3.2 %collective-permute-start.15 = (bf16[512,256]{1,0:T(8,128)(2,1)S(1)}, bf16[512,256]{1,0:T(8,128)(2,1)S(1)}, u32[]{:S(2)}, u32[]{:S(2)}) collective-permute-start(bf16[512,256]{1,0:T(8,128)(2,1)S(1)} %add.94.ka_ref.va_ref), channel_id=1, source_target_pairs={{0,1},{1,0},{2,3},{3,2},{4,5},{5,4},{6,7},{7,6},{8,9},{9,8},{10,11... | collective-permute-start | bytes 786440 | tf_op jit(solution)/shard_map/ppermute | solution.py:75
  48.0 0.7 copy-start.3
  62.0 0.7 copy-start.2
